TPU v7x, 32 devices: a whole 2x2x4 slice. The times are simulated.
32 devices in a mesh: ctx: 4 (over z), tp: 2 (over x), dp: 4 (over y, core).
Axes of the slice: x: 2, y: 2, z: 4, core: 2. Of those that a mesh axis runs over, the one named last changes fastest.
Arguments:
- queries: bfloat16 [4, 1024, 8192], P('dp', 'ctx', 'tp'), may hold values from -80 to 80
- prompt_keys: bfloat16 [4, 1024, 1024], P('dp', 'ctx', 'tp'), may hold values from -4 to 4
- prompt_values: bfloat16 [4, 1024, 1024], P('dp', 'ctx', 'tp'), may hold values from -6 to 6
- resp_keys: bfloat16 [4, 1024, 1024], P('dp', 'ctx', 'tp'), may hold values from -4 to 4
- resp_values: bfloat16 [4, 1024, 1024], P('dp', 'ctx', 'tp'), may hold values from -6 to 6
- pattern: int32 [4, 2, 8], P('dp'), may hold values from 0 to 1, as said below
- lengths: int32 [4, 2], P('dp'), may hold values from 257 to 512, as said below
- out_weight: bfloat16 [8192, 4096], P(('tp', 'dp'), 'ctx'), may hold values from -0.0625 to 0.0625
Outputs:
- attended: bfloat16 [4, 1024, 4096], P('dp', 'ctx', 'tp')
Inputs may be any that keep to these rules, and one draw needn't show every extreme that they name: pattern[g, r, 0] is 1 for every response; each response reads 4 or more blocks; in each group some response reads all 8 blocks. `lengths`: in each group some response has length 512.
All inputs are finite; a program needn't handle non-finite values.
Results may differ from a plain program's by a relative error of at most 0.013.
Values may be sent and summed in bfloat16 or wider, within the bound.
A program may use at most 192 MiB of HBM per device.

v0:
```python
import jax
import jax.numpy as jnp
from jax import lax
from jax.sharding import PartitionSpec as P

HD = 128
BLK = 128
RLEN = 512


def shifted(x, axis, by):
    devices = lax.axis_size(axis)
    pairs = [(i, i + by) for i in range(devices) if 0 <= i + by < devices]
    return lax.ppermute(x, axis, pairs)


def local(
    queries, prompt_keys, prompt_values, resp_keys, resp_values, pattern, lengths, out_weight
):
    tok = queries.shape[1]
    kv_here = prompt_keys.shape[2] // HD
    q_here = queries.shape[2] // HD
    group = q_here // kv_here
    scale = HD ** (-0.5)
    halves = RLEN // tok
    responses = lax.axis_size("ctx") // halves
    place = lax.axis_index("ctx")
    resp_id = place % responses
    half = place // responses
    positions = half * tok + jnp.arange(tok, dtype=jnp.int32)
    chosen = jnp.arange(pattern.shape[1], dtype=jnp.int32) == resp_id
    block_row = jnp.sum(jnp.where(chosen[:, None], pattern[0], 0), axis=0)
    live_len = jnp.sum(jnp.where(chosen, lengths[0], 0))
    query_heads = queries[0].reshape(tok, kv_here, group, HD)
    earlier = shifted((resp_keys, resp_values), "ctx", responses)
    own_keys = jnp.concatenate([earlier[0][0], resp_keys[0]], axis=0).reshape(2 * tok, kv_here, HD)
    own_vals = jnp.concatenate([earlier[1][0], resp_values[0]], axis=0).reshape(
        2 * tok, kv_here, HD
    )
    key_pos = (half - 1) * tok + jnp.arange(2 * tok, dtype=jnp.int32)
    allowed = (key_pos[None, :] >= 0) & (key_pos[None, :] <= positions[:, None])
    scores = (
        jnp.einsum("ikgd,jkd->kgij", query_heads, own_keys, preferred_element_type=jnp.float32)
        * scale
    )
    running = jnp.max(jnp.where(allowed, scores, -jnp.inf), axis=-1)
    probs = jnp.where(allowed, jnp.exp(scores - running[..., None]), 0.0)
    total = jnp.sum(probs, axis=-1)
    accum = jnp.einsum(
        "kgij,jkd->kgid", probs.astype(jnp.bfloat16), own_vals, preferred_element_type=jnp.float32
    )
    pieces = (
        lax.all_gather(prompt_keys, "ctx", axis=1, tiled=True),
        lax.all_gather(prompt_values, "ctx", axis=1, tiled=True),
    )
    count = pieces[0].shape[1]
    block_ids = jnp.arange(count, dtype=jnp.int32) // BLK
    onehot = block_ids[:, None] == jnp.arange(block_row.shape[0], dtype=jnp.int32)[None, :]
    readable = jnp.sum(jnp.where(onehot, block_row[None, :], 0), axis=1) > 0
    piece_keys = pieces[0][0].reshape(-1, kv_here, HD)
    piece_vals = pieces[1][0].reshape(-1, kv_here, HD)
    block_scores = (
        jnp.einsum("ikgd,jkd->kgij", query_heads, piece_keys, preferred_element_type=jnp.float32)
        * scale
    )
    mask = readable[None, None, None, :]
    new_max = jnp.maximum(running, jnp.max(jnp.where(mask, block_scores, -jnp.inf), axis=-1))
    weights = jnp.where(mask, jnp.exp(block_scores - new_max[..., None]), 0.0)
    factor = jnp.exp(running - new_max)
    new_total = total * factor + jnp.sum(weights, axis=-1)
    new_acc = accum * factor[..., None] + jnp.einsum(
        "kgij,jkd->kgid",
        weights.astype(jnp.bfloat16),
        piece_vals,
        preferred_element_type=jnp.float32,
    )
    context = new_acc / new_total[..., None]
    context = jnp.transpose(context, (2, 0, 1, 3)).reshape(tok, q_here * HD)
    context = jnp.where((positions < live_len)[:, None], context, 0.0).astype(jnp.bfloat16)
    head_rows = lax.all_gather(out_weight, "dp", axis=0, tiled=True)
    partial_out = jnp.dot(
        context,
        lax.all_gather(head_rows, "ctx", axis=1, tiled=True),
        preferred_element_type=jnp.float32,
    )
    summed = lax.psum_scatter(
        partial_out.astype(jnp.bfloat16), "tp", scatter_dimension=1, tiled=True
    )
    return summed[None]


def solution(mesh):
    placed = (
        P("dp", "ctx", "tp"),
        P("dp", "ctx", "tp"),
        P("dp", "ctx", "tp"),
        P("dp", "ctx", "tp"),
        P("dp", "ctx", "tp"),
        P("dp", None, None),
        P("dp", None),
        P(("tp", "dp"), "ctx"),
    )
    return jax.shard_map(
        local, mesh=mesh, in_specs=placed, out_specs=P("dp", "ctx", "tp"), check_vma=False
    )
```

profile of v0, /device:TPU:0, one launch (start us, length us, event | category | flops | bytes accessed | tf_op | source)
XLA Modules:
  0.0 758.8 jit_solution(10825526492452625463)
XLA Ops:
  6.5 0.0 all-gather.9.cloned.1.call-start
  6.5 0.7 all-gather.9.cloned.1.call-update
  7.3 0.0 all-gather.5.cloned.1.call-start
  7.3 1.8 copy.37
  9.1 0.0 all-gather.5.cloned.1.call-update
  9.1 0.0 all-gather.7.cloned.1.call-start
  9.2 0.7 all-gather.7.cloned.1.call-update
  9.9 0.0 all-gather.11.cloned.1.call-start
  9.9 60.0 %all-gather.9.cloned.1.call-done = bf16[4096,1024]{1,0:T(8,128)(2,1)} async-done(((bf16[1024,1024]{1,0:T(8,128)(2,1)}), bf16[4096,1024]{1,0:T(8,128)(2,1)}) %all-gather.9.cloned.1.call-update) | async-done | bytes 8388624 | tf_op jit(solution)/shard_map/all_gather | solution.py:80
  69.9 0.0 all-gather.11.cloned.1.call-update
  69.9 0.0 reduce-scatter.2.cloned.1.call-start
  70.0 1.1 copy.29
  71.1 4.3 collective-permute-start
  75.4 1.3 collective-permute-start.1
  76.8 0.6 broadcast_compare_fusion.1
  77.4 1.3 fusion.33
  78.7 0.8 fusion.32
  79.4 0.1 select_reduce_fusion
  79.5 0.6 broadcast_compare_fusion.2
  80.2 1.1 copy.35
  81.3 2.1 copy.50
  83.3 0.2 copy.32
  83.5 0.9 compare_and_fusion
  84.4 0.3 collective-permute-done
  84.7 0.2 copy.31
  84.9 10.4 %collective-permute-done.1 = bf16[1,256,512]{2,1,0:T(8,128)(2,1)S(1)} collective-permute-done((bf16[1,256,512]{2,1,0:T(8,128)(2,1)}, bf16[1,256,512]{2,1,0:T(8,128)(2,1)S(1)}, u32[]{:S(2)}, u32[]{:S(2)}) %collective-permute-start.1) | collective-permute-done | bytes 262176 | tf_op jit(solution)/shard_map/ppermute | solution.py:14
  95.3 0.1 copy.34
  95.5 7.3 fusion.5
  102.7 9.2 %fusion.11 = f32[4,8,256]{2,1,0:T(8,128)S(1)} fusion(f32[4,512,256,8]{2,1,3,0:T(8,128)} %get-tuple-element.8, f32[4,8,256]{2,1,0:T(8,128)S(1)} %get-tuple-element.7, pred[256,512]{0,1:T(8,128)(4,1)S(1)} %compare_and_fusion), kind=kLoop, calls=%fused_computation.14 | loop fusion | flops 16769024 | bytes 16973824 | tf_op jit(solution)/shard_map/reduce_sum | solution.py:48
  111.9 0.6 all-gather.5.cloned.1.call-done
  112.5 16.0 %fusion = (f32[4,8,256]{2,1,0:T(8,128)S(1)}, f32[4,1024,256,8]{2,1,3,0:T(8,128)}) fusion(pred[1024]{0:T(1024)(128)(4,1)S(1)} %broadcast_compare_fusion, bf16[1024,4,128,1]{0,2,3,1:T(8,128)(2,1)} %bitcast.100, bf16[256,4,8,128]{3,2,1,0:T(8,128)(2,1)S(1)} %bitcast.98), kind=kOutput, calls=%fused_computation.2 | convolution fusion | flops 2172641280 | bytes 36733952 | tf_op jit(solution)/shard_map/ikgd,jkd->kgij/dot_general | solution.py:63
  128.5 14.6 %all-gather.7.cloned.1.call-done = bf16[1,1024,512]{2,1,0:T(8,128)(2,1)} async-done(((bf16[1,256,512]{2,1,0:T(8,128)(2,1)}), bf16[1,1024,512]{2,1,0:T(8,128)(2,1)}) %all-gather.7.cloned.1.call-update) | async-done | bytes 1048592 | tf_op jit(solution)/shard_map/all_gather | solution.py:54
  143.1 1.5 copy.40
  144.6 17.4 %fusion.3 = f32[4,8,256]{2,1,0:T(8,128)S(1)} fusion(f32[4,1024,256,8]{2,1,3,0:T(8,128)} %get-tuple-element.10, f32[4,8,256]{2,1,0:T(8,128)S(1)} %max.18, pred[1024]{0:T(1024)(128)(4,1)S(1)} %broadcast_compare_fusion), kind=kLoop, calls=%fused_computation.5 | loop fusion | flops 33546240 | bytes 33620992 | tf_op jit(solution)/shard_map/reduce_sum | solution.py:70
  162.1 16.9 %fusion.8 = f32[4,8,256,128]{2,3,1,0:T(8,128)S(1)} fusion(bf16[1024,4,128,1]{0,2,3,1:T(8,128)(2,1)S(1)} %bitcast.101, f32[4,1024,256,8]{2,1,3,0:T(8,128)} %get-tuple-element.10, f32[4,8,256]{2,1,0:T(8,128)S(1)} %max.18, pred[1024]{0:T(1024)(128)(4,1)S(1)} %broadcast_compare_fusion), kind=kOutput, calls=%fused_computation.12 | convolution fusion | flops 2181038080 | bytes 38831104 | tf_op jit(solution)/shard_map/kgij,jkd->kgid/dot_general | solution.py:71
  178.9 7.8 %fusion.17 = bf16[256,4,8,128]{0,3,2,1:T(8,128)(2,1)S(1)} fusion(f32[4,8,256,128]{2,3,1,0:T(8,128)S(1)} %fusion.8, f32[4,512,256,8]{2,1,3,0:T(8,128)} %get-tuple-element.8, f32[4,8,256]{2,1,0:T(8,128)S(1)} %get-tuple-element.7, pred[256,512]{0,1:T(8,128)(4,1)S(1)} %compare_and_fusion, f32[256,4,8]{0,2,1:T(8,128)S(1)} %get-tuple-element.5, ...), kind=kOutput, calls=%fused_computation.22 | convolution fusion | flops 1095761920 | bytes 23822336 | tf_op jit(solution)/shard_map/kgij,jkd->kgid/dot_general | solution.py:49
  186.8 0.5 fusion.16
  187.3 518.1 %all-gather.11.cloned.1.call-done = bf16[4096,4096]{1,0:T(8,128)(2,1)} async-done(((bf16[4096,1024]{1,0:T(8,128)(2,1)}), bf16[4096,4096]{1,0:T(8,128)(2,1)}) %all-gather.11.cloned.1.call-update) | async-done | bytes 33554448 | tf_op jit(solution)/shard_map/all_gather | solution.py:83
  705.3 16.7 %convolution_convert_fusion = bf16[256,4096]{1,0:T(8,128)(2,1)} fusion(bf16[256,4096]{0,1:T(8,128)(2,1)S(1)} %fusion.16, bf16[4096,4096]{1,0:T(8,128)(2,1)} %all-gather.11.cloned.1.call-done), kind=kOutput, calls=%fused_computation.18 | convolution fusion | flops 8590983168 | bytes 37748736 | tf_op jit(solution)/shard_map/dot_general | solution.py:81
  722.0 0.0 reduce-scatter.2.cloned.1.call-update
  722.1 30.2 %reduce-scatter.2.cloned.1.call-done = bf16[256,2048]{1,0:T(8,128)(2,1)} async-done(((bf16[256,4096]{1,0:T(8,128)(2,1)}), bf16[256,2048]{1,0:T(8,128)(2,1)}) %reduce-scatter.2.cloned.1.call-update) | async-done | bytes 1048592 | tf_op jit(solution)/shard_map/reduce_scatter | solution.py:86
  (7 shorter events, 0.0 us)
Async XLA Ops:
  6.5 63.4 %all-gather.9.cloned.1.call-start = ((), (), s32[]{:S(2)}) async-start(), calls=%async_computation.3 | async-start | bytes 10485760 | tf_op jit(solution)/shard_map/all_gather | solution.py:80
  7.3 105.2 %all-gather.5.cloned.1.call-start = ((), (), s32[]{:S(2)}) async-start(), calls=%async_computation.1 | async-start | bytes 1310720 | tf_op jit(solution)/shard_map/all_gather | solution.py:53
  9.1 134.0 %all-gather.7.cloned.1.call-start = ((), (), s32[]{:S(2)}) async-start(), calls=%async_computation.2 | async-start | bytes 1310720 | tf_op jit(solution)/shard_map/all_gather | solution.py:54
  9.9 695.5 %all-gather.11.cloned.1.call-start = ((), (), s32[]{:S(2)}) async-start(), calls=%async_computation.4 | async-start | bytes 41943040 | tf_op jit(solution)/shard_map/all_gather | solution.py:83
  69.9 682.4 %reduce-scatter.2.cloned.1.call-start = ((), (), s32[]{:S(2)}) async-start(), calls=%async_computation.5 | async-start | bytes 3145728 | tf_op jit(solution)/shard_map/reduce_scatter | solution.py:86
  71.1 13.6 %collective-permute-start = (bf16[1,256,512]{1,2,0:T(8,128)(2,1)S(1)}, bf16[1,256,512]{1,2,0:T(8,128)(2,1)S(1)}, u32[]{:S(2)}, u32[]{:S(2)}) collective-permute-start(bf16[1,256,512]{1,2,0:T(8,128)(2,1)S(1)} %copy.29), channel_id=1, source_target_pairs={{0,16},{8,24},{1,17},{9,25},{2,18},{10,26},{3,19},{11,27},{4,20},{... | collective-permute-start | bytes 786440 | tf_op jit(solution)/shard_map/ppermute | solution.py:14
  75.4 19.9 %collective-permute-start.1 = (bf16[1,256,512]{2,1,0:T(8,128)(2,1)}, bf16[1,256,512]{2,1,0:T(8,128)(2,1)S(1)}, u32[]{:S(2)}, u32[]{:S(2)}) collective-permute-start(bf16[1,256,512]{2,1,0:T(8,128)(2,1)} %param.12), channel_id=1, source_target_pairs={{0,16},{8,24},{1,17},{9,25},{2,18},{10,26},{3,19},{11,27},{4,20},{... | collective-permute-start | bytes 786440 | tf_op jit(solution)/shard_map/ppermute | solution.py:14
Sparse Core Ops, SparseCore 0:
  8.9 60.9 all-gather.8
  71.5 40.9 all-gather.4
  114.1 28.9 all-gather.6
  144.6 560.7 all-gather.10
  722.2 30.0 reduce-scatter.1
where the time goes:
time: 759 us
  waiting for transfers between devices  636 us (84%)
  matrix products  64.6 us (9%)
  other arithmetic  31.4 us (4%)
  between operations  13.3 us (2%)
  local copies, waits for them, and re-layouts  7.98 us (1%)
    all_gather x1, waiting for transfers between devices, local(): lax.all_gather(head_rows, 'ctx', axis=1, tiled=True)  518 us
    all_gather x1, waiting for transfers between devices, local(): head_rows = lax.all_gather(out_weight, 'dp', axis=0, tiled=True)  60 us
    reduce_scatter x1, waiting for transfers between devices, local(): lax.psum_scatter(partial_out.astype(jnp.bfloat16), 'tp', scatter_dimensio...  30.2 us
    reduce_sum x1, other arithmetic, local(): new_total = total * factor + jnp.sum(weights, axis=-1)  17.4 us
    dot_general x1, matrix products, local(): jnp.einsum('kgij,jkd->kgid', weights.astype(jnp.bfloat16), piece_vals, pr...  16.9 us
    dot_general x1, matrix products, local(): jnp.dot(context, lax.all_gather(head_rows, 'ctx', axis=1, tiled=True), pr...  16.7 us
    dot_general x1, matrix products, local(): jnp.einsum('ikgd,jkd->kgij', query_heads, piece_keys, preferred_element_t...  16 us
  transfers between devices with their start and end apart: 7, of which 7 were waited for; matrix products, arithmetic and copies ran while one was open for 12% of the time, Pallas kernels for 0%

commit v1 on v0

--- a/solution.py
+++ b/solution.py
@@ -78,13 +78,11 @@
     context = jnp.transpose(context, (2, 0, 1, 3)).reshape(tok, q_here * HD)
     context = jnp.where((positions < live_len)[:, None], context, 0.0).astype(jnp.bfloat16)
     head_rows = lax.all_gather(out_weight, "dp", axis=0, tiled=True)
-    partial_out = jnp.dot(
-        context,
-        lax.all_gather(head_rows, "ctx", axis=1, tiled=True),
-        preferred_element_type=jnp.float32,
-    )
+    rows = lax.all_gather(context, "ctx", axis=0, tiled=True)
+    columns = jnp.dot(rows, head_rows, preferred_element_type=jnp.float32).astype(jnp.bfloat16)
+    partial_out = lax.all_to_all(columns, "ctx", split_axis=0, concat_axis=1, tiled=True)
     summed = lax.psum_scatter(
-        partial_out.astype(jnp.bfloat16), "tp", scatter_dimension=1, tiled=True
+        partial_out, "tp", scatter_dimension=1, tiled=True
     )
     return summed[None]
 

time: 759 us -> 399 us (0.53)
  waiting for transfers between devices: 636 us -> 228 us
  blocking collectives: 0 us -> 50.8 us
    all_gather x1, waiting for transfers between devices: 518 us -> 151 us  [local(): rows = lax.all_gather(context, 'ctx', axis=0, tiled=True)]
    all_to_all x0 -> x1, blocking collectives: none -> 50.8 us  [local(): lax.all_to_all(columns, 'ctx', split_axis=0, concat_axis=1, tiled=True)]
    all_gather x1, waiting for transfers between devices: 60 us -> 17.9 us  [local(): head_rows = lax.all_gather(out_weight, 'dp', axis=0, tiled=True)]
  transfers between devices with their start and end apart: 7 -> 7, of which waited for: 7 -> 6; matrix products, arithmetic and copies ran while one was open for 12% -> 21% of each run, Pallas kernels for 0% -> 0%
where the time goes in v1:
time: 399 us
  waiting for transfers between devices  228 us (57%)
  matrix products  59.1 us (15%)
  blocking collectives  50.8 us (13%)
  other arithmetic  31 us (8%)
  between operations  13.3 us (3%)
  local copies, waits for them, and re-layouts  9.5 us (2%)
  starting transfers between devices  7.45 us (2%)
    all_gather x1, waiting for transfers between devices, local(): rows = lax.all_gather(context, 'ctx', axis=0, tiled=True)  151 us
    all_to_all x1, blocking collectives, local(): lax.all_to_all(columns, 'ctx', split_axis=0, concat_axis=1, tiled=True)  50.8 us
    reduce_scatter x1, waiting for transfers between devices, local(): lax.psum_scatter(partial_out, 'tp', scatter_dimension=1, tiled=True)  31.3 us
    all_gather x1, waiting for transfers between devices, local(): head_rows = lax.all_gather(out_weight, 'dp', axis=0, tiled=True)  17.9 us
    dot_general x1, matrix products, local(): jnp.einsum('ikgd,jkd->kgij', query_heads, piece_keys, preferred_element_t...  16.1 us
    reduce_sum x1, other arithmetic, local(): new_total = total * factor + jnp.sum(weights, axis=-1)  15.7 us
    all_gather x1, waiting for transfers between devices, local(): lax.all_gather(prompt_values, 'ctx', axis=1, tiled=True)  14.8 us
    dot_general x1, matrix products, local(): jnp.einsum('kgij,jkd->kgid', weights.astype(jnp.bfloat16), piece_vals, pr...  14.2 us
  transfers between devices with their start and end apart: 7, of which 6 were waited for; matrix products, arithmetic and copies ran while one was open for 21% of the time, Pallas kernels for 0%

profile of v1, /device:TPU:0, one launch (start us, length us, event | category | flops | bytes accessed | tf_op | source)
XLA Modules:
  0.0 398.9 jit_solution(16821264540768724130)
XLA Ops:
  6.5 0.0 all-gather.5.cloned.1.call-start
  6.5 1.8 copy.39
  8.3 0.0 all-gather.5.cloned.1.call-update
  8.4 0.0 all-gather.7.cloned.1.call-start
  8.4 0.7 all-gather.7.cloned.1.call-update
  9.1 0.0 all-gather.11.cloned.1.call-start
  9.2 0.7 all-gather.11.cloned.1.call-update
  9.8 0.0 all-gather.9.cloned.1.call-start
  9.9 1.1 copy.31
  11.0 6.0 %collective-permute-start = (bf16[1,256,512]{1,2,0:T(8,128)(2,1)S(1)}, bf16[1,256,512]{1,2,0:T(8,128)(2,1)S(1)}, u32[]{:S(2)}, u32[]{:S(2)}) collective-permute-start(bf16[1,256,512]{1,2,0:T(8,128)(2,1)S(1)} %copy.31), channel_id=1, source_target_pairs={{0,16},{8,24},{1,17},{9,25},{2,18},{10,26},{3,19},{11,27},{4,20},{... | collective-permute-start | bytes 786440 | tf_op jit(solution)/shard_map/ppermute | solution.py:14
  17.0 1.3 collective-permute-start.1
  18.3 0.6 broadcast_compare_fusion.1
  18.9 1.3 fusion.33
  20.2 0.8 fusion.32
  21.0 0.1 select_reduce_fusion
  21.1 0.6 broadcast_compare_fusion.2
  21.7 1.1 copy.37
  22.7 2.1 copy.54
  24.8 0.2 copy.34
  25.0 0.9 compare_and_fusion
  25.9 1.8 collective-permute-done
  27.7 0.2 copy.33
  27.8 10.0 %collective-permute-done.1 = bf16[1,256,512]{2,1,0:T(8,128)(2,1)S(1)} collective-permute-done((bf16[1,256,512]{2,1,0:T(8,128)(2,1)}, bf16[1,256,512]{2,1,0:T(8,128)(2,1)S(1)}, u32[]{:S(2)}, u32[]{:S(2)}) %collective-permute-start.1) | collective-permute-done | bytes 262176 | tf_op jit(solution)/shard_map/ppermute | solution.py:14
  37.9 0.1 copy.36
  38.0 7.2 %fusion.5 = (f32[4,8,256]{2,1,0:T(8,128)S(1)}, f32[4,512,256,8]{2,1,3,0:T(8,128)}) fusion(pred[256,512]{0,1:T(8,128)(4,1)S(1)} %compare_and_fusion, bf16[256,4,8,128]{3,2,1,0:T(8,128)(2,1)S(1)} %bitcast.101, bf16[256,4,128]{2,0,1:T(8,128)(2,1)S(1)} %copy.34, bf16[256,4,128]{2,0,1:T(8,128)(2,1)S(1)} %copy.33), kind=kOutput, calls=%fused_computation.9 | convolution fusion | flops 1087365120 | bytes 19562496 | tf_op jit(solution)/shard_map/ikgd,jkd->kgij/dot_general | solution.py:43
  45.2 9.2 %fusion.11 = f32[4,8,256]{2,1,0:T(8,128)S(1)} fusion(f32[4,512,256,8]{2,1,3,0:T(8,128)} %get-tuple-element.8, f32[4,8,256]{2,1,0:T(8,128)S(1)} %get-tuple-element.7, pred[256,512]{0,1:T(8,128)(4,1)S(1)} %compare_and_fusion), kind=kLoop, calls=%fused_computation.14 | loop fusion | flops 16769024 | bytes 16973824 | tf_op jit(solution)/shard_map/reduce_sum | solution.py:48
  54.3 0.0 all-gather.5.cloned.1.call-done
  54.4 16.1 %fusion = (f32[4,8,256]{2,1,0:T(8,128)S(1)}, f32[4,1024,256,8]{2,1,3,0:T(8,128)}) fusion(pred[1024]{0:T(1024)(128)(4,1)S(1)} %broadcast_compare_fusion, bf16[1024,4,128,1]{0,2,3,1:T(8,128)(2,1)} %bitcast.107, bf16[256,4,8,128]{3,2,1,0:T(8,128)(2,1)S(1)} %bitcast.102), kind=kOutput, calls=%fused_computation.2 | convolution fusion | flops 2172641280 | bytes 36733952 | tf_op jit(solution)/shard_map/ikgd,jkd->kgij/dot_general | solution.py:63
  70.4 14.8 %all-gather.7.cloned.1.call-done = bf16[1,1024,512]{2,1,0:T(8,128)(2,1)} async-done(((bf16[1,256,512]{2,1,0:T(8,128)(2,1)}), bf16[1,1024,512]{2,1,0:T(8,128)(2,1)}) %all-gather.7.cloned.1.call-update) | async-done | bytes 1048592 | tf_op jit(solution)/shard_map/all_gather | solution.py:54
  85.2 1.5 copy.42
  86.7 15.7 %fusion.3 = f32[4,8,256]{2,1,0:T(8,128)S(1)} fusion(f32[4,1024,256,8]{2,1,3,0:T(8,128)} %get-tuple-element.10, f32[4,8,256]{2,1,0:T(8,128)S(1)} %max.18, pred[1024]{0:T(1024)(128)(4,1)S(1)} %broadcast_compare_fusion), kind=kLoop, calls=%fused_computation.5 | loop fusion | flops 33546240 | bytes 33620992 | tf_op jit(solution)/shard_map/reduce_sum | solution.py:70
  102.4 14.2 %fusion.8 = f32[4,8,256,128]{2,3,1,0:T(8,128)S(1)} fusion(bf16[1024,4,128,1]{0,2,3,1:T(8,128)(2,1)S(1)} %bitcast.108, f32[4,1024,256,8]{2,1,3,0:T(8,128)} %get-tuple-element.10, f32[4,8,256]{2,1,0:T(8,128)S(1)} %max.18, pred[1024]{0:T(1024)(128)(4,1)S(1)} %broadcast_compare_fusion), kind=kOutput, calls=%fused_computation.12 | convolution fusion | flops 2181038080 | bytes 38831104 | tf_op jit(solution)/shard_map/kgij,jkd->kgid/dot_general | solution.py:71
  116.6 7.9 %fusion.17 = bf16[256,4,8,128]{0,3,2,1:T(8,128)(2,1)S(1)} fusion(f32[4,8,256,128]{2,3,1,0:T(8,128)S(1)} %fusion.8, f32[4,512,256,8]{2,1,3,0:T(8,128)} %get-tuple-element.8, f32[4,8,256]{2,1,0:T(8,128)S(1)} %get-tuple-element.7, pred[256,512]{0,1:T(8,128)(4,1)S(1)} %compare_and_fusion, f32[256,4,8]{0,2,1:T(8,128)S(1)} %get-tuple-element.5, ...), kind=kOutput, calls=%fused_computation.21 | convolution fusion | flops 1095761920 | bytes 23822336 | tf_op jit(solution)/shard_map/kgij,jkd->kgid/dot_general | solution.py:49
  124.6 1.9 fusion.16
  126.5 0.0 all-gather.9.cloned.1.call-update
  126.5 0.0 reduce-scatter.2.cloned.1.call-start
  126.6 17.9 %all-gather.11.cloned.1.call-done = bf16[4096,1024]{1,0:T(8,128)(2,1)} async-done(((bf16[1024,1024]{1,0:T(8,128)(2,1)}), bf16[4096,1024]{1,0:T(8,128)(2,1)}) %all-gather.11.cloned.1.call-update) | async-done | bytes 8388624 | tf_op jit(solution)/shard_map/all_gather | solution.py:80
  144.5 150.6 %all-gather.9.cloned.1.call-done = bf16[1024,4096]{0,1:T(8,128)(2,1)} async-done(((bf16[256,4096]{0,1:T(8,128)(2,1)}), bf16[1024,4096]{0,1:T(8,128)(2,1)}) %all-gather.9.cloned.1.call-update) | async-done | bytes 8388624 | tf_op jit(solution)/shard_map/all_gather | solution.py:81
  295.0 13.7 %convolution_convert_fusion = bf16[1024,1024]{1,0:T(8,128)(2,1)S(1)} fusion(bf16[1024,4096]{0,1:T(8,128)(2,1)} %all-gather.9.cloned.1.call-done, bf16[4096,1024]{1,0:T(8,128)(2,1)} %all-gather.11.cloned.1.call-done), kind=kOutput, calls=%fused_computation.23 | convolution fusion | flops 8590983168 | bytes 18874368 | tf_op jit(solution)/shard_map/dot_general | solution.py:82
  308.8 50.8 %all_to_all.19 = bf16[4,256,1024]{2,1,0:T(8,128)(2,1)S(1)} all-to-all(bf16[4,256,1024]{2,1,0:T(8,128)(2,1)S(1)} %bitcast.106), channel_id=1, replica_groups=mesh['ctx'=4,'tp'=2,'dp'=4] {'ctx'}, dimensions={0} | all-to-all | bytes 4194304 | tf_op jit(solution)/shard_map/all_to_all | solution.py:83
  359.5 1.5 copy.53
  361.1 0.0 reduce-scatter.2.cloned.1.call-update
  361.1 31.3 %reduce-scatter.2.cloned.1.call-done = bf16[256,2048]{1,0:T(8,128)(2,1)} async-done(((bf16[256,4096]{1,0:T(8,128)(2,1)}), bf16[256,2048]{1,0:T(8,128)(2,1)}) %reduce-scatter.2.cloned.1.call-update) | async-done | bytes 1048592 | tf_op jit(solution)/shard_map/reduce_scatter | solution.py:84
  (7 shorter events, 0.0 us)
Async XLA Ops:
  6.5 47.8 %all-gather.5.cloned.1.call-start = ((), (), s32[]{:S(2)}) async-start(), calls=%async_computation.2 | async-start | bytes 1310720 | tf_op jit(solution)/shard_map/all_gather | solution.py:53
  8.4 76.9 %all-gather.7.cloned.1.call-start = ((), (), s32[]{:S(2)}) async-start(), calls=%async_computation.3 | async-start | bytes 1310720 | tf_op jit(solution)/shard_map/all_gather | solution.py:54
  9.1 135.4 %all-gather.11.cloned.1.call-start = ((), (), s32[]{:S(2)}) async-start(), calls=%async_computation.5 | async-start | bytes 10485760 | tf_op jit(solution)/shard_map/all_gather | solution.py:80
  9.8 285.2 %all-gather.9.cloned.1.call-start = ((), (), s32[]{:S(2)}) async-start(), calls=%async_computation.4 | async-start | bytes 10485760 | tf_op jit(solution)/shard_map/all_gather | solution.py:81
  11.0 16.7 %collective-permute-start = (bf16[1,256,512]{1,2,0:T(8,128)(2,1)S(1)}, bf16[1,256,512]{1,2,0:T(8,128)(2,1)S(1)}, u32[]{:S(2)}, u32[]{:S(2)}) collective-permute-start(bf16[1,256,512]{1,2,0:T(8,128)(2,1)S(1)} %copy.31), channel_id=1, source_target_pairs={{0,16},{8,24},{1,17},{9,25},{2,18},{10,26},{3,19},{11,27},{4,20},{... | collective-permute-start | bytes 786440 | tf_op jit(solution)/shard_map/ppermute | solution.py:14
  17.0 20.9 %collective-permute-start.1 = (bf16[1,256,512]{2,1,0:T(8,128)(2,1)}, bf16[1,256,512]{2,1,0:T(8,128)(2,1)S(1)}, u32[]{:S(2)}, u32[]{:S(2)}) collective-permute-start(bf16[1,256,512]{2,1,0:T(8,128)(2,1)} %param.12), channel_id=1, source_target_pairs={{0,16},{8,24},{1,17},{9,25},{2,18},{10,26},{3,19},{11,27},{4,20},{... | collective-permute-start | bytes 786440 | tf_op jit(solution)/shard_map/ppermute | solution.py:14
  126.5 265.9 %reduce-scatter.2.cloned.1.call-start = ((), (), s32[]{:S(2)}) async-start(), calls=%async_computation.6 | async-start | bytes 3145728 | tf_op jit(solution)/shard_map/reduce_scatter | solution.py:84
Sparse Core Ops, SparseCore 0:
  8.9 44.7 all-gather.4
  55.2 29.9 all-gather.6
  86.8 57.6 all-gather.10
  145.9 149.0 all-gather.8
  361.2 31.1 reduce-scatter.1

commit v2 on v1

v2 whole, which is shorter than its diff:
```python
import jax
import jax.numpy as jnp
from jax import lax
from jax.experimental import pallas as pl
from jax.experimental.pallas import tpu as pltpu
from jax.sharding import PartitionSpec as P

HD = 128
BLK = 128
RLEN = 512


def shifted(x, axis, by):
    devices = lax.axis_size(axis)
    pairs = [(i, i + by) for i in range(devices) if 0 <= i + by < devices]
    return lax.ppermute(x, axis, pairs)


def swapped(x, axis, stride):
    return lax.ppermute(x, axis, [(i, i ^ stride) for i in range(lax.axis_size(axis))])


def attend_head(at_ref, q_ref, k_ref, v_ref, bias_ref, o_ref):
    scores = lax.dot_general(
        q_ref[...], k_ref[...], (((1,), (1,)), ((), ())), preferred_element_type=jnp.float32
    )
    scores = scores * (HD**-0.5) + bias_ref[...]
    probs = jnp.exp(scores - jnp.max(scores, axis=-1, keepdims=True))
    total = jnp.sum(probs, axis=-1, keepdims=True)
    mixed = jnp.dot(probs.astype(jnp.bfloat16), v_ref[...], preferred_element_type=jnp.float32)
    slot = lax.broadcasted_iota(jnp.int32, mixed.shape, 0)
    o_ref[...] = jnp.where(slot < at_ref[1], mixed / total, 0.0).astype(o_ref.dtype)


def attend(at, queries, keys, vals, bias, heads, group):
    tok, count = bias.shape
    return pl.pallas_call(
        attend_head,
        grid_spec=pltpu.PrefetchScalarGridSpec(
            num_scalar_prefetch=1,
            grid=(heads,),
            in_specs=[
                pl.BlockSpec((tok, HD), lambda h, at: (0, at[0] + h)),
                pl.BlockSpec((count, HD), lambda h, at: (0, (at[0] + h) // group)),
                pl.BlockSpec((count, HD), lambda h, at: (0, (at[0] + h) // group)),
                pl.BlockSpec((tok, count), lambda h, at: (0, 0)),
            ],
            out_specs=pl.BlockSpec((tok, HD), lambda h, at: (0, h)),
        ),
        out_shape=jax.ShapeDtypeStruct((tok, heads * HD), jnp.bfloat16),
        cost_estimate=pl.CostEstimate(
            flops=4 * heads * tok * count * HD,
            bytes_accessed=4 * heads * tok * HD + 4 * count * HD + 4 * tok * count,
            transcendentals=heads * tok * count,
        ),
    )(at, queries, keys, vals, bias)


def local(
    queries, prompt_keys, prompt_values, resp_keys, resp_values, pattern, lengths, out_weight
):
    tok = queries.shape[1]
    width = prompt_keys.shape[2]
    group = queries.shape[2] // width
    heads = out_weight.shape[0] // HD
    halves = RLEN // tok
    places = lax.axis_size("ctx")
    responses = places // halves
    place = lax.axis_index("ctx")
    resp_id = place % responses
    half = place // responses

    prompt = lax.all_gather(
        jnp.concatenate([prompt_keys[0], prompt_values[0]], axis=1), "ctx", axis=0, tiled=True
    )
    own = jnp.concatenate([resp_keys[0], resp_values[0]], axis=1)
    earlier = shifted(own, "ctx", responses)

    blocks = {(0, 0): out_weight}
    stride = 2
    while stride < places:
        blocks.update({(k ^ stride, j): swapped(b, "ctx", stride) for (k, j), b in blocks.items()})
        stride *= 2
    stride = lax.axis_size("dp") // 2
    while stride:
        blocks.update({(k, j ^ stride): swapped(b, "dp", stride) for (k, j), b in blocks.items()})
        stride //= 2

    chosen = jnp.arange(pattern.shape[1], dtype=jnp.int32) == resp_id
    block_row = jnp.sum(jnp.where(chosen[:, None], pattern[0], 0), axis=0)
    live_len = jnp.sum(jnp.where(chosen, lengths[0], 0))
    readable = jnp.repeat(block_row, BLK) > 0
    positions = half * tok + jnp.arange(tok, dtype=jnp.int32)
    key_pos = (half - 1) * tok + jnp.arange(2 * tok, dtype=jnp.int32)
    allowed = (key_pos[None, :] >= 0) & (key_pos[None, :] <= positions[:, None])
    allowed = jnp.concatenate(
        [jnp.broadcast_to(readable[None, :], (tok, readable.shape[0])), allowed], axis=1
    )
    bias = jnp.where(allowed, 0.0, -jnp.inf).astype(jnp.float32)
    both = jnp.concatenate([prompt, earlier, own], axis=0)
    keys, vals = both[:, :width], both[:, width:]

    sums = {}
    for j in sorted({j for _, j in blocks}, key=lambda j: (j & 1, j)):
        first = (lax.axis_index("dp") ^ j) * heads
        at = jnp.stack([first, live_len - half * tok]).astype(jnp.int32)
        context = attend(at, queries[0], keys, vals, bias, heads, group)
        rows = jnp.concatenate([context, swapped(context, "ctx", 1)], axis=0)
        for k in sorted({k for k, _ in blocks}):
            term = jnp.dot(rows, blocks[k, j], preferred_element_type=jnp.float32)
            sums[k] = sums[k] + term if k in sums else term
    mine = {}
    for k, total in sums.items():
        total = total.astype(jnp.bfloat16)
        mine[k] = total[:tok]
        mine[k ^ 1] = swapped(total[tok:], "ctx", 1)
    stacked = jnp.stack([mine[k] for k in range(places)])
    partial_out = jnp.concatenate(
        [lax.dynamic_index_in_dim(stacked, b ^ place, 0, keepdims=False) for b in range(places)],
        axis=1,
    )
    summed = lax.psum_scatter(partial_out, "tp", scatter_dimension=1, tiled=True)
    return summed[None]


def solution(mesh):
    placed = (
        P("dp", "ctx", "tp"),
        P("dp", "ctx", "tp"),
        P("dp", "ctx", "tp"),
        P("dp", "ctx", "tp"),
        P("dp", "ctx", "tp"),
        P("dp", None, None),
        P("dp", None),
        P(("tp", "dp"), "ctx"),
    )
    return jax.shard_map(
        local, mesh=mesh, in_specs=placed, out_specs=P("dp", "ctx", "tp"), check_vma=False
    )
```

time: 399 us -> 324 us (0.81)
  blocking collectives: 50.8 us -> 0 us
  Pallas kernels: 0 us -> 42.8 us
  waiting for transfers between devices: 228 us -> 187 us
  matrix products: 59.1 us -> 20.1 us
  starting transfers between devices: 7.45 us -> 35.4 us
  other arithmetic: 31 us -> 21.5 us
  local copies, waits for them, and re-layouts: 9.5 us -> 2.35 us
    all_gather x4 -> x1, waiting for transfers between devices: 183 us -> 0.01 us  [local(): lax.all_gather(jnp.concatenate([prompt_keys[0], prompt_values[0]], axis=1...]
    ppermute x0 -> x13, waiting for transfers between devices: none -> 155 us  [swapped(): lax.ppermute(x, axis, [(i, i ^ stride) for i in range(lax.axis_size(axis))])]
    all_to_all x1 -> x0, blocking collectives: 50.8 us -> none  [local(): lax.all_to_all(columns, 'ctx', split_axis=0, concat_axis=1, tiled=True)]
    pallas_call x0 -> x4, Pallas kernels: none -> 42.8 us  [attend(): pl.pallas_call(attend_head, grid_spec=pltpu.PrefetchScalarGridSpec(num_sc...]
    dot_general x5 -> x8, matrix products: 59.1 us -> 20.1 us  [local(): term = jnp.dot(rows, blocks[k, j], preferred_element_type=jnp.float32)]
    ppermute x0 -> x13, starting transfers between devices: none -> 33.1 us  [swapped(): lax.ppermute(x, axis, [(i, i ^ stride) for i in range(lax.axis_size(axis))])]
    reduce_sum x3 -> x0, other arithmetic: 24.9 us -> none  [the longest x1 15.7 us: local(): new_total = total * factor + jnp.sum(weights, axis=-1)]
    concatenate x0 -> x4, other arithmetic: none -> 16.5 us  [the longest x1 11.2 us: local(): both = jnp.concatenate([prompt, earlier, own], axis=0)]
  transfers between devices with their start and end apart: 7 -> 16, of which waited for: 6 -> 8; matrix products, arithmetic and copies ran while one was open for 21% -> 12% of each run, Pallas kernels for 0% -> 13%
where the time goes in v2:
time: 324 us; the launch traced here: 323 us
  waiting for transfers between devices  187 us (58%)
  Pallas kernels  42.8 us (13%)
  starting transfers between devices  35.4 us (11%)
  other arithmetic  21.5 us (7%)
  matrix products  20.1 us (6%)
  between operations  14.2 us (4%)
    ppermute x13, waiting for transfers between devices, swapped(): lax.ppermute(x, axis, [(i, i ^ stride) for i in range(lax.axis_size(axis))])  155 us
    pallas_call x4, Pallas kernels, attend(): pl.pallas_call(attend_head, grid_spec=pltpu.PrefetchScalarGridSpec(num_sc...  42.8 us
    ppermute x13, starting transfers between devices, swapped(): lax.ppermute(x, axis, [(i, i ^ stride) for i in range(lax.axis_size(axis))])  33.1 us
    reduce_scatter x1, waiting for transfers between devices, local(): lax.psum_scatter(partial_out, 'tp', scatter_dimension=1, tiled=True)  32 us
    dot_general x8, matrix products, local(): term = jnp.dot(rows, blocks[k, j], preferred_element_type=jnp.float32)  20.1 us
    concatenate x1, other arithmetic, local(): both = jnp.concatenate([prompt, earlier, own], axis=0)  11.2 us
  transfers between devices with their start and end apart: 16, of which 8 were waited for; matrix products, arithmetic and copies ran while one was open for 12% of the time, Pallas kernels for 13%

profile of v2, /device:TPU:0, one launch (start us, length us, event | category | flops | bytes accessed | tf_op | source)
XLA Modules:
  0.0 323.2 jit_solution(8315018812162479085)
XLA Ops:
  6.6 2.0 pad_maximum_fusion.14
  8.5 0.0 all-gather.2.cloned.1.call-update
  8.5 0.0 reduce-scatter.2.cloned.1.call-start
  8.6 3.1 collective-permute-start.3
  11.6 0.0 collective-permute-start.5
  11.6 2.6 collective-permute-start.9
  14.2 1.9 pad_maximum_fusion.15
  16.1 2.3 collective-permute-start
  18.4 0.0 copy-done.6
  18.4 0.1 fusion.6
  18.5 0.1 broadcast_bitcast_fusion
  18.6 0.0 copy-done.7
  18.6 0.6 fusion.7
  19.9 0.6 pad_add_fusion.1.at_ref
  20.5 0.6 pad_add_fusion.at_ref
  21.1 0.2 compare_and_fusion
  21.2 1.3 add_select_fusion.bias_ref
  22.6 0.6 pad_add_fusion.2.at_ref
  23.2 34.4 %collective-permute-done.3 = bf16[1024,1024]{1,0:T(8,128)(2,1)} collective-permute-done((bf16[1024,1024]{1,0:T(8,128)(2,1)}, bf16[1024,1024]{1,0:T(8,128)(2,1)}, u32[]{:S(2)}, u32[]{:S(2)}) %collective-permute-start.3) | collective-permute-done | bytes 2097184 | tf_op jit(solution)/shard_map/ppermute | solution.py:20
  57.6 0.0 collective-permute-start.7
  57.6 82.0 %collective-permute-done.9 = bf16[1024,1024]{1,0:T(8,128)(2,1)} collective-permute-done((bf16[1024,1024]{1,0:T(8,128)(2,1)}, bf16[1024,1024]{1,0:T(8,128)(2,1)}, u32[]{:S(2)}, u32[]{:S(2)}) %collective-permute-start.9) | collective-permute-done | bytes 2097184 | tf_op jit(solution)/shard_map/ppermute | solution.py:20
  139.6 0.5 collective-permute-start.10
  140.0 0.0 collective-permute-done
  140.1 11.2 %maximum_maximum_fusion = bf16[1536,1024]{1,0:T(8,128)(2,1)S(1)} fusion(bf16[256,512]{1,0:T(8,128)(2,1)S(1)} %bitcast.48, bf16[256,512]{1,0:T(8,128)(2,1)S(1)} %bitcast.50, bf16[256,1024]{1,0:T(8,128)(2,1)S(1)} %collective-permute-done, bf16[1024,1024]{1,0:T(8,128)(2,1)} %all-gather.2.cloned.1.call-done), kind=kLoop, calls=%fused_computation | loop fusion | flops 12582912 | bytes 6291456 | tf_op jit(solution)/shard_map/concatenate | solution.py:100
  151.2 1.9 fusion.16
  153.2 10.7 %shard_map.82 = bf16[256,1024]{1,0:T(8,128)(2,1)} custom-call(s32[2]{0:T(128)} %pad_add_fusion.at_ref, bf16[256,4096]{1,0:T(8,128)(2,1)} %bitcast.43, bf16[1536,512]{1,0:T(8,128)(2,1)} %get-tuple-element.6.k_ref, bf16[1536,512]{1,0:T(8,128)(2,1)} %get-tuple-element.5.v_ref, f32[256,1536]{1,0:T(8,128)} %add_select_fusion.bias_ref), custom_call_target="tpu_custom_call" | custom-call | flops 1610612736 | bytes 3407872 | tf_op jit(solution)/shard_map/pallas_call | solution.py:37
  163.8 22.6 %collective-permute-start.1 = (bf16[256,1024]{1,0:T(8,128)(2,1)}, bf16[256,1024]{1,0:T(8,128)(2,1)}, u32[]{:S(2)}, u32[]{:S(2)}) collective-permute-start(bf16[256,1024]{1,0:T(8,128)(2,1)} %shard_map.82), channel_id=1, source_target_pairs={{0,8},{8,0},{16,24},{24,16},{1,9},{9,1},{17,25},{25,17},{2,10},{10... | collective-permute-start | bytes 1572872 | tf_op jit(solution)/shard_map/ppermute | solution.py:20
  186.5 0.6 pad_add_fusion.3.at_ref
  187.1 0.0 collective-permute-start.11
  187.1 10.7 %shard_map.83 = bf16[256,1024]{1,0:T(8,128)(2,1)} custom-call(s32[2]{0:T(128)} %pad_add_fusion.1.at_ref, bf16[256,4096]{1,0:T(8,128)(2,1)} %bitcast.44, bf16[1536,512]{1,0:T(8,128)(2,1)} %get-tuple-element.6.k_ref, bf16[1536,512]{1,0:T(8,128)(2,1)} %get-tuple-element.5.v_ref, f32[256,1536]{1,0:T(8,128)} %add_select_fusion.bias_ref), custom_call_target="tpu_custom_call" | custom-call | flops 1610612736 | bytes 3407872 | tf_op jit(solution)/shard_map/pallas_call | solution.py:37
  197.8 10.7 %shard_map.84 = bf16[256,1024]{1,0:T(8,128)(2,1)} custom-call(s32[2]{0:T(128)} %pad_add_fusion.2.at_ref, bf16[256,4096]{1,0:T(8,128)(2,1)} %bitcast.45, bf16[1536,512]{1,0:T(8,128)(2,1)} %get-tuple-element.6.k_ref, bf16[1536,512]{1,0:T(8,128)(2,1)} %get-tuple-element.5.v_ref, f32[256,1536]{1,0:T(8,128)} %add_select_fusion.bias_ref), custom_call_target="tpu_custom_call" | custom-call | flops 1610612736 | bytes 3407872 | tf_op jit(solution)/shard_map/pallas_call | solution.py:37
  208.5 10.7 %shard_map.85 = bf16[256,1024]{1,0:T(8,128)(2,1)} custom-call(s32[2]{0:T(128)} %pad_add_fusion.3.at_ref, bf16[256,4096]{1,0:T(8,128)(2,1)} %bitcast.46, bf16[1536,512]{1,0:T(8,128)(2,1)} %get-tuple-element.6.k_ref, bf16[1536,512]{1,0:T(8,128)(2,1)} %get-tuple-element.5.v_ref, f32[256,1536]{1,0:T(8,128)} %add_select_fusion.bias_ref), custom_call_target="tpu_custom_call" | custom-call | flops 1610612736 | bytes 3407872 | tf_op jit(solution)/shard_map/pallas_call | solution.py:37
  219.2 0.0 collective-permute-done.1
  219.2 0.1 collective-permute-start.2
  219.4 3.0 fusion.5
  222.4 0.0 collective-permute-done.5
  222.4 2.0 collective-permute-start.4
  224.5 3.0 fusion.4
  227.5 6.6 %collective-permute-done.2 = bf16[256,1024]{1,0:T(8,128)(2,1)S(1)} collective-permute-done((bf16[256,1024]{1,0:T(8,128)(2,1)S(1)}, bf16[256,1024]{1,0:T(8,128)(2,1)S(1)}, u32[]{:S(2)}, u32[]{:S(2)}) %collective-permute-start.2) | collective-permute-done | bytes 524320 | tf_op jit(solution)/shard_map/ppermute | solution.py:20
  234.1 0.1 collective-permute-start.6
  234.2 0.0 collective-permute-done.10
  234.2 0.0 collective-permute-start.12
  234.2 2.8 fusion.3
  237.0 8.3 %collective-permute-done.4 = bf16[256,1024]{1,0:T(8,128)(2,1)S(1)} collective-permute-done((bf16[256,1024]{1,0:T(8,128)(2,1)S(1)}, bf16[256,1024]{1,0:T(8,128)(2,1)S(1)}, u32[]{:S(2)}, u32[]{:S(2)}) %collective-permute-start.4) | collective-permute-done | bytes 524320 | tf_op jit(solution)/shard_map/ppermute | solution.py:20
  245.3 2.9 fusion.1
  248.2 7.9 %collective-permute-done.6 = bf16[256,1024]{1,0:T(8,128)(2,1)S(1)} collective-permute-done((bf16[256,1024]{1,0:T(8,128)(2,1)S(1)}, bf16[256,1024]{1,0:T(8,128)(2,1)S(1)}, u32[]{:S(2)}, u32[]{:S(2)}) %collective-permute-start.6) | collective-permute-done | bytes 524320 | tf_op jit(solution)/shard_map/ppermute | solution.py:20
  256.1 0.0 collective-permute-done.7
  256.1 1.3 add_convert_fusion.1
  257.5 0.1 slice_bitcast_fusion.1
  257.5 0.4 collective-permute-start.8
  257.9 2.8 fusion.2
  260.7 0.0 collective-permute-done.11
  260.8 2.9 fusion
  263.6 0.0 collective-permute-done.12
  263.6 1.3 add_convert_fusion
  264.9 0.1 slice_bitcast_fusion
  265.0 1.8 collective-permute-start.13
  266.8 5.6 %collective-permute-done.8 = bf16[256,1024]{1,0:T(8,128)(2,1)S(1)} collective-permute-done((bf16[256,1024]{1,0:T(8,128)(2,1)S(1)}, bf16[256,1024]{1,0:T(8,128)(2,1)S(1)}, u32[]{:S(2)}, u32[]{:S(2)}) %collective-permute-start.8) | collective-permute-done | bytes 524320 | tf_op jit(solution)/shard_map/ppermute | solution.py:20
  272.4 9.9 %collective-permute-done.13 = bf16[256,1024]{1,0:T(8,128)(2,1)S(1)} collective-permute-done((bf16[256,1024]{1,0:T(8,128)(2,1)S(1)}, bf16[256,1024]{1,0:T(8,128)(2,1)S(1)}, u32[]{:S(2)}, u32[]{:S(2)}) %collective-permute-start.13) | collective-permute-done | bytes 524320 | tf_op jit(solution)/shard_map/ppermute | solution.py:20
  282.3 0.3 pad_maximum_fusion
  282.6 0.2 dynamic-slice_bitcast_fusion.3
  282.8 1.5 pad_maximum_fusion.1
  284.3 0.0 reduce-scatter.2.cloned.1.call-update
  284.3 32.0 %reduce-scatter.2.cloned.1.call-done = bf16[256,2048]{1,0:T(8,128)(2,1)} async-done(((bf16[256,4096]{1,0:T(8,128)(2,1)}), bf16[256,2048]{1,0:T(8,128)(2,1)}) %reduce-scatter.2.cloned.1.call-update) | async-done | bytes 1048592 | tf_op jit(solution)/shard_map/reduce_scatter | solution.py:122
  (22 shorter events, 0.1 us)
Async XLA Ops:
  6.5 11.9 %copy-start.6 = (s32[1,2,8]{2,1,0:T(2,128)S(1)}, s32[1,2,8]{2,1,0:T(2,128)}, u32[]{:S(2)}) copy-start(s32[1,2,8]{2,1,0:T(2,128)} %param.13) | copy-start | bytes 196
  6.5 12.1 %copy-start.7 = (s32[1,2]{1,0:T(1,128)S(1)}, s32[1,2]{1,0:T(1,128)}, u32[]{:S(2)}) copy-start(s32[1,2]{1,0:T(1,128)} %param.14) | copy-start | bytes 28
  6.5 133.5 %all-gather.2.cloned.1.call-start = ((), (), s32[]{:S(2)}) async-start(), calls=%async_computation.1 | async-start | bytes 2621440 | tf_op jit(solution)/shard_map/all_gather | solution.py:73
  6.5 133.5 %copy-start.1 = (bf16[1,256,512]{2,1,0:T(8,128)(2,1)S(1)}, bf16[1,256,512]{2,1,0:T(8,128)(2,1)}, u32[]{:S(2)}) copy-start(bf16[1,256,512]{2,1,0:T(8,128)(2,1)} %param.12) | copy-start | bytes 786436
  6.5 133.5 %copy-start.2 = (bf16[1,256,512]{2,1,0:T(8,128)(2,1)S(1)}, bf16[1,256,512]{2,1,0:T(8,128)(2,1)}, u32[]{:S(2)}) copy-start(bf16[1,256,512]{2,1,0:T(8,128)(2,1)} %param.11) | copy-start | bytes 786436
  8.5 307.8 %reduce-scatter.2.cloned.1.call-start = ((), (), s32[]{:S(2)}) async-start(), calls=%async_computation.2 | async-start | bytes 3145728 | tf_op jit(solution)/shard_map/reduce_scatter | solution.py:122
  8.6 49.0 %collective-permute-start.3 = (bf16[1024,1024]{1,0:T(8,128)(2,1)}, bf16[1024,1024]{1,0:T(8,128)(2,1)}, u32[]{:S(2)}, u32[]{:S(2)}) collective-permute-start(bf16[1024,1024]{1,0:T(8,128)(2,1)} %param.15), channel_id=1, source_target_pairs={{0,2},{1,3},{2,0},{3,1},{4,6},{5,7},{6,4},{7,5},{8,10},{9,11},{10,... | collective-permute-start | bytes 6291464 | tf_op jit(solution)/shard_map/ppermute | solution.py:20
  11.6 210.8 %collective-permute-start.5 = (bf16[1024,1024]{1,0:T(8,128)(2,1)}, bf16[1024,1024]{1,0:T(8,128)(2,1)}, u32[]{:S(2)}, u32[]{:S(2)}) collective-permute-start(bf16[1024,1024]{1,0:T(8,128)(2,1)} %param.15), channel_id=1, source_target_pairs={{0,1},{1,0},{2,3},{3,2},{4,5},{5,4},{6,7},{7,6},{8,9},{9,8},{10,11... | collective-permute-start | bytes 6291464 | tf_op jit(solution)/shard_map/ppermute | solution.py:20
  11.6 127.9 %collective-permute-start.9 = (bf16[1024,1024]{1,0:T(8,128)(2,1)}, bf16[1024,1024]{1,0:T(8,128)(2,1)}, u32[]{:S(2)}, u32[]{:S(2)}) collective-permute-start(bf16[1024,1024]{1,0:T(8,128)(2,1)} %param.15), channel_id=1, source_target_pairs={{0,16},{8,24},{16,0},{24,8},{1,17},{9,25},{17,1},{25,9},{2,18},{10... | collective-permute-start | bytes 6291464 | tf_op jit(solution)/shard_map/ppermute | solution.py:20
  16.1 123.9 %collective-permute-start = (bf16[256,1024]{1,0:T(8,128)(2,1)}, bf16[256,1024]{1,0:T(8,128)(2,1)S(1)}, u32[]{:S(2)}, u32[]{:S(2)}) collective-permute-start(bf16[256,1024]{1,0:T(8,128)(2,1)} %pad_maximum_fusion.15), channel_id=1, source_target_pairs={{0,16},{8,24},{1,17},{9,25},{2,18},{10,26},{3,19},{11,27},{4,20},{... | collective-permute-start | bytes 1572872 | tf_op jit(solution)/shard_map/ppermute | solution.py:16
  57.6 198.5 %collective-permute-start.7 = (bf16[1024,1024]{1,0:T(8,128)(2,1)}, bf16[1024,1024]{1,0:T(8,128)(2,1)S(1)}, u32[]{:S(2)}, u32[]{:S(2)}) collective-permute-start(bf16[1024,1024]{1,0:T(8,128)(2,1)} %collective-permute-done.3), channel_id=1, source_target_pairs={{0,1},{1,0},{2,3},{3,2},{4,5},{5,4},{6,7},{7,6},{8,9},{9,8},{10,11... | collective-permute-start | bytes 6291464 | tf_op jit(solution)/shard_map/ppermute | solution.py:20
  139.6 94.6 %collective-permute-start.10 = (bf16[1024,1024]{1,0:T(8,128)(2,1)}, bf16[1024,1024]{1,0:T(8,128)(2,1)}, u32[]{:S(2)}, u32[]{:S(2)}) collective-permute-start(bf16[1024,1024]{1,0:T(8,128)(2,1)} %collective-permute-done.9), channel_id=1, source_target_pairs={{0,2},{1,3},{2,0},{3,1},{4,6},{5,7},{6,4},{7,5},{8,10},{9,11},{10,... | collective-permute-start | bytes 6291464 | tf_op jit(solution)/shard_map/ppermute | solution.py:20
  163.8 55.4 %collective-permute-start.1 = (bf16[256,1024]{1,0:T(8,128)(2,1)}, bf16[256,1024]{1,0:T(8,128)(2,1)}, u32[]{:S(2)}, u32[]{:S(2)}) collective-permute-start(bf16[256,1024]{1,0:T(8,128)(2,1)} %shard_map.82), channel_id=1, source_target_pairs={{0,8},{8,0},{16,24},{24,16},{1,9},{9,1},{17,25},{25,17},{2,10},{10... | collective-permute-start | bytes 1572872 | tf_op jit(solution)/shard_map/ppermute | solution.py:20
  187.1 73.6 %collective-permute-start.11 = (bf16[1024,1024]{1,0:T(8,128)(2,1)}, bf16[1024,1024]{1,0:T(8,128)(2,1)}, u32[]{:S(2)}, u32[]{:S(2)}) collective-permute-start(bf16[1024,1024]{1,0:T(8,128)(2,1)} %collective-permute-done.9), channel_id=1, source_target_pairs={{0,1},{1,0},{2,3},{3,2},{4,5},{5,4},{6,7},{7,6},{8,9},{9,8},{10,11... | collective-permute-start | bytes 6291464 | tf_op jit(solution)/shard_map/ppermute | solution.py:20
  208.5 10.7 %copy-start.4 = (bf16[256,1024]{1,0:T(8,128)(2,1)S(1)}, bf16[256,1024]{1,0:T(8,128)(2,1)}, u32[]{:S(2)}) copy-start(bf16[256,1024]{1,0:T(8,128)(2,1)} %shard_map.83) | copy-start | bytes 1572868
  208.5 10.9 %copy-start.5 = (bf16[256,1024]{1,0:T(8,128)(2,1)S(1)}, bf16[256,1024]{1,0:T(8,128)(2,1)}, u32[]{:S(2)}) copy-start(bf16[256,1024]{1,0:T(8,128)(2,1)} %shard_map.82) | copy-start | bytes 1572868
  219.2 3.2 copy-start.3
  219.2 14.9 %collective-permute-start.2 = (bf16[256,1024]{1,0:T(8,128)(2,1)S(1)}, bf16[256,1024]{1,0:T(8,128)(2,1)S(1)}, u32[]{:S(2)}, u32[]{:S(2)}) collective-permute-start(bf16[256,1024]{1,0:T(8,128)(2,1)S(1)} %copy-done.4), channel_id=1, source_target_pairs={{0,8},{8,0},{16,24},{24,16},{1,9},{9,1},{17,25},{25,17},{2,10},{10... | collective-permute-start | bytes 1572872 | tf_op jit(solution)/shard_map/ppermute | solution.py:20
  222.4 11.7 %copy-start = (bf16[256,1024]{1,0:T(8,128)(2,1)S(1)}, bf16[256,1024]{1,0:T(8,128)(2,1)}, u32[]{:S(2)}) copy-start(bf16[256,1024]{1,0:T(8,128)(2,1)} %shard_map.85) | copy-start | bytes 1572868
  222.4 22.9 %collective-permute-start.4 = (bf16[256,1024]{1,0:T(8,128)(2,1)S(1)}, bf16[256,1024]{1,0:T(8,128)(2,1)S(1)}, u32[]{:S(2)}, u32[]{:S(2)}) collective-permute-start(bf16[256,1024]{1,0:T(8,128)(2,1)S(1)} %copy-done.3), channel_id=1, source_target_pairs={{0,8},{8,0},{16,24},{24,16},{1,9},{9,1},{17,25},{25,17},{2,10},{10... | collective-permute-start | bytes 1572872 | tf_op jit(solution)/shard_map/ppermute | solution.py:20
  234.1 22.0 %collective-permute-start.6 = (bf16[256,1024]{1,0:T(8,128)(2,1)S(1)}, bf16[256,1024]{1,0:T(8,128)(2,1)S(1)}, u32[]{:S(2)}, u32[]{:S(2)}) collective-permute-start(bf16[256,1024]{1,0:T(8,128)(2,1)S(1)} %copy-done), channel_id=1, source_target_pairs={{0,8},{8,0},{16,24},{24,16},{1,9},{9,1},{17,25},{25,17},{2,10},{10... | collective-permute-start | bytes 1572872 | tf_op jit(solution)/shard_map/ppermute | solution.py:20
  234.2 29.4 %collective-permute-start.12 = (bf16[1024,1024]{1,0:T(8,128)(2,1)}, bf16[1024,1024]{1,0:T(8,128)(2,1)S(1)}, u32[]{:S(2)}, u32[]{:S(2)}) collective-permute-start(bf16[1024,1024]{1,0:T(8,128)(2,1)} %collective-permute-done.10), channel_id=1, source_target_pairs={{0,1},{1,0},{2,3},{3,2},{4,5},{5,4},{6,7},{7,6},{8,9},{9,8},{10,11... | collective-permute-start | bytes 6291464 | tf_op jit(solution)/shard_map/ppermute | solution.py:20
  257.5 14.9 %collective-permute-start.8 = (bf16[256,1024]{1,0:T(8,128)(2,1)S(1)}, bf16[256,1024]{1,0:T(8,128)(2,1)S(1)}, u32[]{:S(2)}, u32[]{:S(2)}) collective-permute-start(bf16[256,1024]{1,0:T(8,128)(2,1)S(1)} %get-tuple-element.12), channel_id=1, source_target_pairs={{0,8},{8,0},{16,24},{24,16},{1,9},{9,1},{17,25},{25,17},{2,10},{10... | collective-permute-start | bytes 1572872 | tf_op jit(solution)/shard_map/ppermute | solution.py:20
  265.0 17.3 %collective-permute-start.13 = (bf16[256,1024]{1,0:T(8,128)(2,1)S(1)}, bf16[256,1024]{1,0:T(8,128)(2,1)S(1)}, u32[]{:S(2)}, u32[]{:S(2)}) collective-permute-start(bf16[256,1024]{1,0:T(8,128)(2,1)S(1)} %get-tuple-element.14), channel_id=1, source_target_pairs={{0,8},{8,0},{16,24},{24,16},{1,9},{9,1},{17,25},{25,17},{2,10},{10... | collective-permute-start | bytes 1572872 | tf_op jit(solution)/shard_map/ppermute | solution.py:20
Sparse Core Ops, SparseCore 0:
  8.9 101.0 all-gather.1
  284.4 31.8 reduce-scatter.1
